TPU v7x, 512 devices: a whole 4x4x16 slice. The times are simulated.
512 devices in a mesh: rows: 64 (over z, y), cols: 8 (over x, core).
Axes of the slice: x: 4, y: 4, z: 16, core: 2. Of those that a mesh axis runs over, the one named last changes fastest.
Arguments:
- sens_base: bfloat16 [524288, 1024], P('rows', 'cols'), may hold values from -0.14157282 to 0.14157282
- design_field: float32 [512, 1024], P('rows'), may hold values from -3 to 3
- gradient: bfloat16 [512, 1024], P('rows'), may hold values from -6 to 6
- tile_index: int32 [1024], P('cols'), may hold values from 0 to 31
- type_codes: int32 [1024], P('cols'), may hold values from 0 to 2
Outputs:
- r_panels: float32 [512, 1024], P(None, 'cols')
- multipliers: float32 [512], replicated
Inputs may be any that keep to these rules, and one draw needn't show every extreme that they name: `tile_index`: each constraint names one support tile.
All inputs are finite; a program needn't handle non-finite values.
Results may differ from a plain program's by a relative error of at most 0.0003.
The roundings to bfloat16 on the way count: a program that leaves them out, or rounds other values in their place, can miss the bound.
Values may be sent and summed in bfloat16 or wider, within the bound.
A program may use at most 64 MiB of HBM per device.

v0:
```python
import math
import jax
import jax.numpy as jnp
from jax import lax
from jax.sharding import PartitionSpec as P

TILE = 128
PW = 256


def padded_2(cells, sides, width):
    for axis, dim in sides:
        count = lax.axis_size(axis)
        ends = count - 1
        head = lax.slice_in_dim(cells, 0, width, axis=dim)
        tail = lax.slice_in_dim(cells, cells.shape[dim] - width, cells.shape[dim], axis=dim)
        cells = jnp.concatenate(
            [
                lax.ppermute(tail, axis, [(i, (i + 1) % count) for i in range(ends)]),
                cells,
                lax.ppermute(head, axis, [((i + 1) % count, i) for i in range(ends)]),
            ],
            axis=dim,
        )
    return cells


def assemble(base_cols, tile_cols, type_cols, stencils, cell_tile):
    kinds_all = jnp.arange(3, dtype=jnp.int32)
    chooser = (type_cols[None, :] == kinds_all[:, None]).astype(jnp.float32)
    picked = lax.dot_general(
        stencils,
        chooser,
        (((0,), (0,)), ((), ())),
        precision=lax.Precision.HIGHEST,
        preferred_element_type=jnp.float32,
    )
    inside = cell_tile[:, None] == tile_cols[None, :]
    total = base_cols.astype(jnp.float32) + jnp.where(inside, picked / TILE, 0.0)
    return total.astype(jnp.bfloat16)


def matmul(left, right):
    return jnp.dot(left, right, precision=lax.Precision.HIGHEST, preferred_element_type=jnp.float32)


def small_factor(matrix):
    order = matrix.shape[0]
    positions = jnp.arange(order, dtype=jnp.int32)

    def column_step(index_col, carry):
        working, lower = carry
        column = lax.dynamic_slice_in_dim(working, index_col, 1, 1)[:, 0]
        pivot = jnp.sqrt(lax.dynamic_slice_in_dim(column, index_col, 1, 0)[0])
        column = jnp.where(positions >= index_col, column / pivot, 0.0)
        lower = jnp.where(positions[None, :] == index_col, column[:, None], lower)
        working = working - column[:, None] * column[None, :]
        return (working, lower)

    return lax.fori_loop(0, order, column_step, (matrix, jnp.zeros_like(matrix)))[1]


def small_inverse(lower):
    order = lower.shape[0]
    positions = jnp.arange(order, dtype=jnp.int32)
    right = jnp.eye(order, dtype=jnp.float32)

    def row_step(index_row, carry):
        rest, solved = carry
        column = lax.dynamic_slice_in_dim(lower, index_row, 1, 1)[:, 0]
        pivot = lax.dynamic_slice_in_dim(column, index_row, 1, 0)[0]
        value = lax.dynamic_slice_in_dim(rest, index_row, 1, 0) / pivot
        solved = jnp.where(positions[:, None] == index_row, value, solved)
        below = jnp.where(positions > index_row, column, 0.0)
        rest = rest - below[:, None] * value
        return (rest, solved)

    return lax.fori_loop(0, order, row_step, (right, jnp.zeros_like(right)))[1]


def factor_lower(matrix):
    order = matrix.shape[0]
    width = math.gcd(order, 32)
    working = matrix
    lower = jnp.zeros_like(matrix)
    inverses = []
    for block_num in range(order // width):
        start = block_num * width
        diag_lower = small_factor(working[:width, :width])
        diag_inverse = small_inverse(diag_lower)
        inverses.append(diag_inverse)
        lower = lower.at[start : start + width, start : start + width].set(diag_lower)
        if start + width < order:
            panel = matmul(working[width:, :width], diag_inverse.T)
            lower = lower.at[start + width :, start : start + width].set(panel)
            working = working[width:, width:] - matmul(panel, panel.T)
    return (lower, inverses)


def solve_forward(lower, inverses, right):
    width = inverses[0].shape[0]
    solved = []
    for block_num in range(len(inverses)):
        start = block_num * width
        rest = right[start : start + width]
        if block_num > 0:
            rest = rest - matmul(
                lower[start : start + width, :start], jnp.concatenate(solved, axis=0)
            )
        solved.append(matmul(inverses[block_num], rest))
    return jnp.concatenate(solved, axis=0)


def solve_backward(lower, inverses, right):
    width = inverses[0].shape[0]
    order = lower.shape[0]
    solved = []
    for block_num in reversed(range(len(inverses))):
        start = block_num * width
        rest = right[start : start + width]
        if start + width < order:
            rest = rest - matmul(
                lower[start + width :, start : start + width].T, jnp.concatenate(solved, axis=0)
            )
        solved.insert(0, matmul(inverses[block_num].T, rest))
    return jnp.concatenate(solved, axis=0)


def shards(sens_base, design_field, gradient, tile_index, type_codes):
    rows_here = design_field.shape[0]
    grid_width = design_field.shape[1]
    cols_here = sens_base.shape[1]
    factored = 2 * PW
    padded = padded_2(design_field, (("rows", 0),), 1)
    padded = jnp.pad(padded, ((0, 0), (1, 1)))
    north_cells = padded[:-2, 1:-1]
    south_cells = padded[2:, 1:-1]
    west_cells = padded[1:-1, :-2]
    east_cells = padded[1:-1, 2:]
    laplace = 4.0 * design_field - (north_cells + south_cells + west_cells + east_cells)
    slope_x = 0.5 * (east_cells - west_cells)
    slope_y = 0.5 * (south_cells - north_cells)
    stencils = jnp.stack([laplace, slope_x, slope_y]).reshape(3, -1)
    row_glob = lax.axis_index("rows") * rows_here + jnp.arange(rows_here, dtype=jnp.int32)
    col_ids = jnp.arange(grid_width, dtype=jnp.int32) // TILE
    cell_tile = ((row_glob // TILE)[:, None] * (grid_width // TILE) + col_ids[None, :]).reshape(-1)
    local_jac = assemble(sens_base, tile_index, type_codes, stencils, cell_tile)
    grad_flat = gradient.reshape(-1)
    row_major = lax.all_to_all(local_jac, "cols", split_axis=0, concat_axis=1, tiled=True)
    row_piece = row_major.shape[0]
    grad_part = lax.dynamic_slice_in_dim(
        grad_flat, lax.axis_index("cols") * row_piece, row_piece, 0
    )
    leading = row_major[:, :factored]
    gram_block = lax.dot_general(
        leading, row_major, (((0,), (0,)), ((), ())), preferred_element_type=jnp.float32
    )
    projected = jnp.dot(grad_part, leading, preferred_element_type=jnp.float32)
    gram_block, projected = lax.psum((gram_block, projected), ("rows", "cols"))
    gram_head = gram_block[:, :factored]
    gram_own = lax.dynamic_slice_in_dim(
        gram_block, lax.axis_index("cols") * cols_here, cols_here, 1
    )
    lower_chol, inverses = factor_lower(gram_head)
    r_panels = solve_forward(lower_chol, inverses, gram_own)
    half_solved = solve_forward(lower_chol, inverses, projected[:, None])
    multipliers = solve_backward(lower_chol, inverses, half_solved)[:, 0]
    return (r_panels, multipliers)


def solution(mesh):
    placed = (P("rows", "cols"), P("rows", None), P("rows", None), P("cols"), P("cols"))
    return jax.shard_map(
        shards, mesh=mesh, in_specs=placed, out_specs=(P(None, "cols"), P()), check_vma=False
    )
```

profile of v0, /device:TPU:1, one launch (start us, length us, event | category | flops | bytes accessed | tf_op | source)
XLA Modules:
  0.0 2140.8 jit_solution(14819654451309352459)
XLA Ops:
  8.1 4.0 collective-permute-start
  13.5 2.9 collective-permute-done.1
  18.4 6.7 fusion.98
  25.0 2.9 copy.37
  27.9 34.2 %all_to_all.19 = bf16[8,1024,128]{1,2,0:T(8,128)(2,1)S(1)} all-to-all(bf16[8,1024,128]{1,2,0:T(8,128)(2,1)S(1)} %copy.37), channel_id=1, replica_groups=mesh['rows'=64,'cols'=8] {'cols'}, dimensions={0} | all-to-all | bytes 4194304 | tf_op jit(solution)/shard_map/all_to_all | solution.py:149
  63.4 2.6 fusion.161
  68.0 110.2 %psum.15 = f32[512]{0:T(512)S(1)} all-reduce(f32[512]{0:T(512)S(1)} %bitcast.1236), channel_id=1, replica_groups=mesh['rows'=64,'cols'=8] {'rows','cols'}, use_global_device_ids=true, to_apply=%region_65.66 | all-reduce | flops 512 | bytes 4096 | tf_op jit(solution)/shard_map/psum | solution.py:159
  178.3 367.6 %all-reduce.4.cloned.1.call-done = f32[512,1024]{1,0:T(8,128)} async-done(((f32[512,1024]{1,0:T(8,128)}), f32[512,1024]{1,0:T(8,128)}) %all-reduce.4.cloned.1.call-update) | async-done | bytes 2097168 | tf_op jit(solution)/shard_map/psum | solution.py:159
  546.7 45.5 %while.671 = (s32[]{:T(128)}, f32[32,32]{0,1:T(8,128)S(1)}, f32[32,32]{0,1:T(8,128)S(1)}, s32[]{:T(128)}, s32[]{:T(128)}, /*index=5*/s32[]{:T(128)}) while((s32[]{:T(128)}, f32[32,32]{0,1:T(8,128)S(1)}, f32[32,32]{0,1:T(8,128)S(1)}, s32[]{:T(128)}, s32[]{:T(128)}, /*index=5*/s32[]{:T(128)}) %tuple.1741), condition=%wide.region_2.3_spmd.clone.clone, body=%wide.region_1.2_spmd.clone.clone.sunk | while | flops 4292 | bytes 19003 | solution.py:60
  592.2 43.6 %while.672 = (s32[]{:T(128)}, f32[32,32]{1,0:T(8,128)S(1)}, f32[32,32]{1,0:T(8,128)S(1)}, f32[32,32]{0,1:T(8,128)S(1)}, s32[]{:T(128)}, /*index=5*/s32[]{:T(128)}, s32[]{:T(128)}) while((s32[]{:T(128)}, f32[32,32]{1,0:T(8,128)S(1)}, f32[32,32]{1,0:T(8,128)S(1)}, f32[32,32]{0,1:T(8,128)S(1)}, s32[]{:T(128)}, ...), condition=%wide.region_4.5_spmd.clone.clone, body=%wide.region_3.4_spmd.clone.clone.sunk | while | flops 4228 | bytes 18367 | solution.py:78
  637.2 2.3 convolution_subtract_fusion
  639.5 45.0 %while.673 = (s32[]{:T(128)}, f32[32,32]{0,1:T(8,128)S(1)}, f32[32,32]{0,1:T(8,128)S(1)}, s32[]{:T(128)}, s32[]{:T(128)}, /*index=5*/s32[]{:T(128)}) while((s32[]{:T(128)}, f32[32,32]{0,1:T(8,128)S(1)}, f32[32,32]{0,1:T(8,128)S(1)}, s32[]{:T(128)}, s32[]{:T(128)}, /*index=5*/s32[]{:T(128)}) %tuple.1747), condition=%wide.region_6.7_spmd.clone.clone, body=%wide.region_5.6_spmd.clone.clone.sunk | while | flops 4292 | bytes 19003 | solution.py:60
  684.6 43.6 %while.674 = (s32[]{:T(128)}, f32[32,32]{1,0:T(8,128)S(1)}, f32[32,32]{1,0:T(8,128)S(1)}, f32[32,32]{0,1:T(8,128)S(1)}, s32[]{:T(128)}, /*index=5*/s32[]{:T(128)}, s32[]{:T(128)}) while((s32[]{:T(128)}, f32[32,32]{1,0:T(8,128)S(1)}, f32[32,32]{1,0:T(8,128)S(1)}, f32[32,32]{0,1:T(8,128)S(1)}, s32[]{:T(128)}, ...), condition=%wide.region_8.9_spmd.clone.clone, body=%wide.region_7.8_spmd.clone.clone.sunk | while | flops 4228 | bytes 18367 | solution.py:78
  729.6 45.0 %while.675 = (s32[]{:T(128)}, f32[32,32]{0,1:T(8,128)S(1)}, f32[32,32]{0,1:T(8,128)S(1)}, s32[]{:T(128)}, s32[]{:T(128)}, /*index=5*/s32[]{:T(128)}) while((s32[]{:T(128)}, f32[32,32]{0,1:T(8,128)S(1)}, f32[32,32]{0,1:T(8,128)S(1)}, s32[]{:T(128)}, s32[]{:T(128)}, /*index=5*/s32[]{:T(128)}) %tuple.1753), condition=%wide.region_10.11_spmd.clone.clone, body=%wide.region_9.10_spmd.clone.clone.sunk | while | flops 4292 | bytes 19003 | solution.py:60
  774.6 43.6 %while.676 = (s32[]{:T(128)}, f32[32,32]{1,0:T(8,128)S(1)}, f32[32,32]{1,0:T(8,128)S(1)}, f32[32,32]{0,1:T(8,128)S(1)}, s32[]{:T(128)}, /*index=5*/s32[]{:T(128)}, s32[]{:T(128)}) while((s32[]{:T(128)}, f32[32,32]{1,0:T(8,128)S(1)}, f32[32,32]{1,0:T(8,128)S(1)}, f32[32,32]{0,1:T(8,128)S(1)}, s32[]{:T(128)}, ...), condition=%wide.region_12.13_spmd.clone.clone, body=%wide.region_11.12_spmd.clone.clone.sunk | while | flops 4228 | bytes 18367 | solution.py:78
  819.6 86.6 %while.677 = (s32[]{:T(128)}, f32[32,32]{0,1:T(8,128)S(1)}, f32[32,32]{0,1:T(8,128)}, s32[]{:T(128)}, s32[]{:T(128)}, /*index=5*/s32[]{:T(128)}) while((s32[]{:T(128)}, f32[32,32]{0,1:T(8,128)S(1)}, f32[32,32]{0,1:T(8,128)}, s32[]{:T(128)}, s32[]{:T(128)}, /*index=5*/s32[]{:T(128)}) %tuple.1759), condition=%wide.region_14.15_spmd.clone.clone, body=%wide.region_13.14_spmd.clone.clone.sunk | while | flops 4292 | bytes 19003 | solution.py:60
  825.7 1.4 select_select_fusion.70
  906.4 1.4 scatter.101
  907.8 2.1 scatter.104
  909.9 1.4 scatter.105
  911.3 2.1 scatter.106
  913.4 1.4 scatter.109
  914.8 2.1 scatter.110
  917.0 86.4 %while.678 = (s32[]{:T(128)}, f32[32,32]{1,0:T(8,128)S(1)}, f32[32,32]{1,0:T(8,128)S(1)}, f32[32,32]{0,1:T(8,128)}, s32[]{:T(128)}, /*index=5*/s32[]{:T(128)}, s32[]{:T(128)}) while((s32[]{:T(128)}, f32[32,32]{1,0:T(8,128)S(1)}, f32[32,32]{1,0:T(8,128)S(1)}, f32[32,32]{0,1:T(8,128)}, s32[]{:T(128)}, ...), condition=%wide.region_16.17_spmd.clone.clone, body=%wide.region_15.16_spmd.clone.clone.sunk | while | flops 4228 | bytes 18751 | solution.py:78
  1004.5 45.0 %while.679 = (s32[]{:T(128)}, f32[32,32]{0,1:T(8,128)S(1)}, f32[32,32]{0,1:T(8,128)S(1)}, s32[]{:T(128)}, s32[]{:T(128)}, /*index=5*/s32[]{:T(128)}) while((s32[]{:T(128)}, f32[32,32]{0,1:T(8,128)S(1)}, f32[32,32]{0,1:T(8,128)S(1)}, s32[]{:T(128)}, s32[]{:T(128)}, /*index=5*/s32[]{:T(128)}) %tuple.1856), condition=%wide.region_18.19_spmd.clone.clone, body=%wide.region_17.18_spmd.clone.clone.sunk | while | flops 4292 | bytes 19003 | solution.py:60
  1049.5 43.6 %while.680 = (s32[]{:T(128)}, f32[32,32]{1,0:T(8,128)S(1)}, f32[32,32]{1,0:T(8,128)S(1)}, f32[32,32]{0,1:T(8,128)S(1)}, s32[]{:T(128)}, /*index=5*/s32[]{:T(128)}, s32[]{:T(128)}) while((s32[]{:T(128)}, f32[32,32]{1,0:T(8,128)S(1)}, f32[32,32]{1,0:T(8,128)S(1)}, f32[32,32]{0,1:T(8,128)S(1)}, s32[]{:T(128)}, ...), condition=%wide.region_20.21_spmd.clone.clone, body=%wide.region_19.20_spmd.clone.clone.sunk | while | flops 4228 | bytes 18367 | solution.py:78
  1094.1 45.0 %while.681 = (s32[]{:T(128)}, f32[32,32]{0,1:T(8,128)S(1)}, f32[32,32]{0,1:T(8,128)S(1)}, s32[]{:T(128)}, s32[]{:T(128)}, /*index=5*/s32[]{:T(128)}) while((s32[]{:T(128)}, f32[32,32]{0,1:T(8,128)S(1)}, f32[32,32]{0,1:T(8,128)S(1)}, s32[]{:T(128)}, s32[]{:T(128)}, /*index=5*/s32[]{:T(128)}) %tuple.1855), condition=%wide.region_22.23_spmd.clone.clone, body=%wide.region_21.22_spmd.clone.clone.sunk | while | flops 4292 | bytes 19003 | solution.py:60
  1139.2 43.6 %while.682 = (s32[]{:T(128)}, f32[32,32]{1,0:T(8,128)S(1)}, f32[32,32]{1,0:T(8,128)S(1)}, f32[32,32]{0,1:T(8,128)S(1)}, s32[]{:T(128)}, /*index=5*/s32[]{:T(128)}, s32[]{:T(128)}) while((s32[]{:T(128)}, f32[32,32]{1,0:T(8,128)S(1)}, f32[32,32]{1,0:T(8,128)S(1)}, f32[32,32]{0,1:T(8,128)S(1)}, s32[]{:T(128)}, ...), condition=%wide.region_24.25_spmd.clone.clone, body=%wide.region_23.24_spmd.clone.clone.sunk | while | flops 4228 | bytes 18367 | solution.py:78
  1183.8 45.0 %while.683 = (s32[]{:T(128)}, f32[32,32]{0,1:T(8,128)S(1)}, f32[32,32]{0,1:T(8,128)S(1)}, s32[]{:T(128)}, s32[]{:T(128)}, /*index=5*/s32[]{:T(128)}) while((s32[]{:T(128)}, f32[32,32]{0,1:T(8,128)S(1)}, f32[32,32]{0,1:T(8,128)S(1)}, s32[]{:T(128)}, s32[]{:T(128)}, /*index=5*/s32[]{:T(128)}) %tuple.1854), condition=%wide.region_26.27_spmd.clone.clone, body=%wide.region_25.26_spmd.clone.clone.sunk | while | flops 4292 | bytes 19003 | solution.py:60
  1228.8 43.6 %while.684 = (s32[]{:T(128)}, f32[32,32]{1,0:T(8,128)S(1)}, f32[32,32]{1,0:T(8,128)S(1)}, f32[32,32]{0,1:T(8,128)S(1)}, s32[]{:T(128)}, /*index=5*/s32[]{:T(128)}, s32[]{:T(128)}) while((s32[]{:T(128)}, f32[32,32]{1,0:T(8,128)S(1)}, f32[32,32]{1,0:T(8,128)S(1)}, f32[32,32]{0,1:T(8,128)S(1)}, s32[]{:T(128)}, ...), condition=%wide.region_28.29_spmd.clone.clone, body=%wide.region_27.28_spmd.clone.clone.sunk | while | flops 4228 | bytes 18367 | solution.py:78
  1273.3 45.0 %while.685 = (s32[]{:T(128)}, f32[32,32]{0,1:T(8,128)S(1)}, f32[32,32]{0,1:T(8,128)S(1)}, s32[]{:T(128)}, s32[]{:T(128)}, /*index=5*/s32[]{:T(128)}) while((s32[]{:T(128)}, f32[32,32]{0,1:T(8,128)S(1)}, f32[32,32]{0,1:T(8,128)S(1)}, s32[]{:T(128)}, s32[]{:T(128)}, /*index=5*/s32[]{:T(128)}) %tuple.1853), condition=%wide.region_30.31_spmd.clone.clone, body=%wide.region_29.30_spmd.clone.clone.sunk | while | flops 4292 | bytes 19003 | solution.py:60
  1326.6 43.6 %while.686 = (s32[]{:T(128)}, f32[32,32]{1,0:T(8,128)S(1)}, f32[32,32]{1,0:T(8,128)S(1)}, f32[32,32]{0,1:T(8,128)S(1)}, s32[]{:T(128)}, /*index=5*/s32[]{:T(128)}, s32[]{:T(128)}) while((s32[]{:T(128)}, f32[32,32]{1,0:T(8,128)S(1)}, f32[32,32]{1,0:T(8,128)S(1)}, f32[32,32]{0,1:T(8,128)S(1)}, s32[]{:T(128)}, ...), condition=%wide.region_32.33_spmd.clone.clone, body=%wide.region_31.32_spmd.clone.clone.sunk | while | flops 4228 | bytes 18367 | solution.py:78
  1371.0 45.0 %while.687 = (s32[]{:T(128)}, f32[32,32]{0,1:T(8,128)S(1)}, f32[32,32]{0,1:T(8,128)S(1)}, s32[]{:T(128)}, s32[]{:T(128)}, /*index=5*/s32[]{:T(128)}) while((s32[]{:T(128)}, f32[32,32]{0,1:T(8,128)S(1)}, f32[32,32]{0,1:T(8,128)S(1)}, s32[]{:T(128)}, s32[]{:T(128)}, /*index=5*/s32[]{:T(128)}) %tuple.1789), condition=%wide.region_34.35_spmd.clone.clone, body=%wide.region_33.34_spmd.clone.clone.sunk | while | flops 4292 | bytes 19003 | solution.py:60
  1416.1 43.6 %while.688 = (s32[]{:T(128)}, f32[32,32]{1,0:T(8,128)S(1)}, f32[32,32]{1,0:T(8,128)S(1)}, f32[32,32]{0,1:T(8,128)S(1)}, s32[]{:T(128)}, /*index=5*/s32[]{:T(128)}, s32[]{:T(128)}) while((s32[]{:T(128)}, f32[32,32]{1,0:T(8,128)S(1)}, f32[32,32]{1,0:T(8,128)S(1)}, f32[32,32]{0,1:T(8,128)S(1)}, s32[]{:T(128)}, ...), condition=%wide.region_36.37_spmd.clone.clone, body=%wide.region_35.36_spmd.clone.clone.sunk | while | flops 4228 | bytes 18367 | solution.py:78
  1460.5 45.0 %while.689 = (s32[]{:T(128)}, f32[32,32]{0,1:T(8,128)S(1)}, f32[32,32]{0,1:T(8,128)S(1)}, s32[]{:T(128)}, s32[]{:T(128)}, /*index=5*/s32[]{:T(128)}) while((s32[]{:T(128)}, f32[32,32]{0,1:T(8,128)S(1)}, f32[32,32]{0,1:T(8,128)S(1)}, s32[]{:T(128)}, s32[]{:T(128)}, /*index=5*/s32[]{:T(128)}) %tuple.1795), condition=%wide.region_38.39_spmd.clone.clone, body=%wide.region_37.38_spmd.clone.clone.sunk | while | flops 4292 | bytes 19003 | solution.py:60
  1505.5 43.6 %while.690 = (s32[]{:T(128)}, f32[32,32]{1,0:T(8,128)S(1)}, f32[32,32]{1,0:T(8,128)S(1)}, f32[32,32]{0,1:T(8,128)S(1)}, s32[]{:T(128)}, /*index=5*/s32[]{:T(128)}, s32[]{:T(128)}) while((s32[]{:T(128)}, f32[32,32]{1,0:T(8,128)S(1)}, f32[32,32]{1,0:T(8,128)S(1)}, f32[32,32]{0,1:T(8,128)S(1)}, s32[]{:T(128)}, ...), condition=%wide.region_40.41_spmd.clone.clone, body=%wide.region_39.40_spmd.clone.clone.sunk | while | flops 4228 | bytes 18367 | solution.py:78
  1549.8 45.0 %while.691 = (s32[]{:T(128)}, f32[32,32]{0,1:T(8,128)S(1)}, f32[32,32]{0,1:T(8,128)S(1)}, s32[]{:T(128)}, s32[]{:T(128)}, /*index=5*/s32[]{:T(128)}) while((s32[]{:T(128)}, f32[32,32]{0,1:T(8,128)S(1)}, f32[32,32]{0,1:T(8,128)S(1)}, s32[]{:T(128)}, s32[]{:T(128)}, /*index=5*/s32[]{:T(128)}) %tuple.1801), condition=%wide.region_42.43_spmd.clone.clone, body=%wide.region_41.42_spmd.clone.clone.sunk | while | flops 4292 | bytes 19003 | solution.py:60
  1594.9 43.6 %while.692 = (s32[]{:T(128)}, f32[32,32]{1,0:T(8,128)S(1)}, f32[32,32]{1,0:T(8,128)S(1)}, f32[32,32]{0,1:T(8,128)S(1)}, s32[]{:T(128)}, /*index=5*/s32[]{:T(128)}, s32[]{:T(128)}) while((s32[]{:T(128)}, f32[32,32]{1,0:T(8,128)S(1)}, f32[32,32]{1,0:T(8,128)S(1)}, f32[32,32]{0,1:T(8,128)S(1)}, s32[]{:T(128)}, ...), condition=%wide.region_44.45_spmd.clone.clone, body=%wide.region_43.44_spmd.clone.clone.sunk | while | flops 4228 | bytes 18367 | solution.py:78
  1639.2 45.0 %while.693 = (s32[]{:T(128)}, f32[32,32]{0,1:T(8,128)S(1)}, f32[32,32]{0,1:T(8,128)S(1)}, s32[]{:T(128)}, s32[]{:T(128)}, /*index=5*/s32[]{:T(128)}) while((s32[]{:T(128)}, f32[32,32]{0,1:T(8,128)S(1)}, f32[32,32]{0,1:T(8,128)S(1)}, s32[]{:T(128)}, s32[]{:T(128)}, /*index=5*/s32[]{:T(128)}) %tuple.1807), condition=%wide.region_46.47_spmd.clone.clone, body=%wide.region_45.46_spmd.clone.clone.sunk | while | flops 4292 | bytes 19003 | solution.py:60
  1691.8 43.6 %while.694 = (s32[]{:T(128)}, f32[32,32]{1,0:T(8,128)S(1)}, f32[32,32]{1,0:T(8,128)S(1)}, f32[32,32]{0,1:T(8,128)S(1)}, s32[]{:T(128)}, /*index=5*/s32[]{:T(128)}, s32[]{:T(128)}) while((s32[]{:T(128)}, f32[32,32]{1,0:T(8,128)S(1)}, f32[32,32]{1,0:T(8,128)S(1)}, f32[32,32]{0,1:T(8,128)S(1)}, s32[]{:T(128)}, ...), condition=%wide.region_48.49_spmd.clone.clone, body=%wide.region_47.48_spmd.clone.clone.sunk | while | flops 4228 | bytes 18367 | solution.py:78
  1736.0 45.0 %while.695 = (s32[]{:T(128)}, f32[32,32]{0,1:T(8,128)S(1)}, f32[32,32]{0,1:T(8,128)S(1)}, s32[]{:T(128)}, s32[]{:T(128)}, /*index=5*/s32[]{:T(128)}) while((s32[]{:T(128)}, f32[32,32]{0,1:T(8,128)S(1)}, f32[32,32]{0,1:T(8,128)S(1)}, s32[]{:T(128)}, s32[]{:T(128)}, /*index=5*/s32[]{:T(128)}) %tuple.1813), condition=%wide.region_50.51_spmd.clone.clone, body=%wide.region_49.50_spmd.clone.clone.sunk | while | flops 4292 | bytes 19003 | solution.py:60
  1781.0 43.6 %while.696 = (s32[]{:T(128)}, f32[32,32]{1,0:T(8,128)S(1)}, f32[32,32]{1,0:T(8,128)S(1)}, f32[32,32]{0,1:T(8,128)S(1)}, s32[]{:T(128)}, /*index=5*/s32[]{:T(128)}, s32[]{:T(128)}) while((s32[]{:T(128)}, f32[32,32]{1,0:T(8,128)S(1)}, f32[32,32]{1,0:T(8,128)S(1)}, f32[32,32]{0,1:T(8,128)S(1)}, s32[]{:T(128)}, ...), condition=%wide.region_52.53_spmd.clone.clone, body=%wide.region_51.52_spmd.clone.clone.sunk | while | flops 4228 | bytes 18367 | solution.py:78
  1825.1 45.0 %while.697 = (s32[]{:T(128)}, f32[32,32]{0,1:T(8,128)S(1)}, f32[32,32]{0,1:T(8,128)S(1)}, s32[]{:T(128)}, s32[]{:T(128)}, /*index=5*/s32[]{:T(128)}) while((s32[]{:T(128)}, f32[32,32]{0,1:T(8,128)S(1)}, f32[32,32]{0,1:T(8,128)S(1)}, s32[]{:T(128)}, s32[]{:T(128)}, /*index=5*/s32[]{:T(128)}) %tuple.1819), condition=%wide.region_54.55_spmd.clone.clone, body=%wide.region_53.54_spmd.clone.clone.sunk | while | flops 4292 | bytes 19003 | solution.py:60
  1870.2 43.6 %while.698 = (s32[]{:T(128)}, f32[32,32]{1,0:T(8,128)S(1)}, f32[32,32]{1,0:T(8,128)S(1)}, f32[32,32]{0,1:T(8,128)S(1)}, s32[]{:T(128)}, /*index=5*/s32[]{:T(128)}, s32[]{:T(128)}) while((s32[]{:T(128)}, f32[32,32]{1,0:T(8,128)S(1)}, f32[32,32]{1,0:T(8,128)S(1)}, f32[32,32]{0,1:T(8,128)S(1)}, s32[]{:T(128)}, ...), condition=%wide.region_56.57_spmd.clone.clone, body=%wide.region_55.56_spmd.clone.clone.sunk | while | flops 4228 | bytes 18367 | solution.py:78
  1914.3 45.0 %while.699 = (s32[]{:T(128)}, f32[32,32]{0,1:T(8,128)S(1)}, f32[32,32]{0,1:T(8,128)S(1)}, s32[]{:T(128)}, s32[]{:T(128)}, /*index=5*/s32[]{:T(128)}) while((s32[]{:T(128)}, f32[32,32]{0,1:T(8,128)S(1)}, f32[32,32]{0,1:T(8,128)S(1)}, s32[]{:T(128)}, s32[]{:T(128)}, /*index=5*/s32[]{:T(128)}) %tuple.1825), condition=%wide.region_58.59_spmd.clone.clone, body=%wide.region_57.58_spmd.clone.clone.sunk | while | flops 4292 | bytes 19003 | solution.py:60
  1959.4 43.6 %while.700 = (s32[]{:T(128)}, f32[32,32]{1,0:T(8,128)S(1)}, f32[32,32]{1,0:T(8,128)S(1)}, f32[32,32]{0,1:T(8,128)S(1)}, s32[]{:T(128)}, /*index=5*/s32[]{:T(128)}, s32[]{:T(128)}) while((s32[]{:T(128)}, f32[32,32]{1,0:T(8,128)S(1)}, f32[32,32]{1,0:T(8,128)S(1)}, f32[32,32]{0,1:T(8,128)S(1)}, s32[]{:T(128)}, ...), condition=%wide.region_60.61_spmd.clone.clone, body=%wide.region_59.60_spmd.clone.clone.sunk | while | flops 4228 | bytes 18367 | solution.py:78
  2016.5 45.0 %while.701 = (s32[]{:T(128)}, f32[32,32]{0,1:T(8,128)S(1)}, f32[32,32]{0,1:T(8,128)S(1)}, s32[]{:T(128)}, s32[]{:T(128)}, /*index=5*/s32[]{:T(128)}) while((s32[]{:T(128)}, f32[32,32]{0,1:T(8,128)S(1)}, f32[32,32]{0,1:T(8,128)S(1)}, s32[]{:T(128)}, s32[]{:T(128)}, /*index=5*/s32[]{:T(128)}) %tuple.1857), condition=%wide.region_62.63_spmd.clone.clone, body=%wide.region_61.62_spmd.clone.clone.sunk | while | flops 4292 | bytes 19003 | solution.py:60
  2061.5 43.6 %while.702 = (s32[]{:T(128)}, f32[32,32]{1,0:T(8,128)S(1)}, f32[32,32]{1,0:T(8,128)S(1)}, f32[32,32]{0,1:T(8,128)S(1)}, s32[]{:T(128)}, /*index=5*/s32[]{:T(128)}, s32[]{:T(128)}) while((s32[]{:T(128)}, f32[32,32]{1,0:T(8,128)S(1)}, f32[32,32]{1,0:T(8,128)S(1)}, f32[32,32]{0,1:T(8,128)S(1)}, s32[]{:T(128)}, ...), condition=%wide.region_64.65_spmd.clone.clone, body=%wide.region_63.64_spmd.clone.clone.sunk | while | flops 4228 | bytes 18367 | solution.py:78
  (5422 shorter events, 1197.8 us)
Async XLA Ops:
  7.2 538.7 %all-reduce.4.cloned.1.call-start = ((), (), s32[]{:S(2)}) async-start(), calls=%async_computation.1 | async-start | bytes 4194304 | tf_op jit(solution)/shard_map/psum | solution.py:159
  8.1 5.4 collective-permute-start
  12.1 4.4 collective-permute-start.1
  62.1 1.3 copy-start.15
  66.1 0.7 copy-start.24
  66.1 1.6 copy-start.16
  66.1 573.3 %copy-start = (f32[32,32]{1,0:T(8,128)}, f32[32,32]{1,0:T(8,128)S(1)}, u32[]{:S(2)}) copy-start(f32[32,32]{1,0:T(8,128)S(1)} %fusion.258) | copy-start | bytes 12292
  639.5 135.1 %copy-start.2 = (f32[32,32]{1,0:T(8,128)S(1)}, f32[32,32]{1,0:T(8,128)}, u32[]{:S(2)}) copy-start(f32[32,32]{1,0:T(8,128)} %copy-done) | copy-start | bytes 12292
  728.2 91.3 %copy-start.22 = (f32[32,32]{0,1:T(8,128)}, f32[32,32]{0,1:T(8,128)S(1)}, u32[]{:S(2)}) copy-start(f32[32,32]{0,1:T(8,128)S(1)} %get-tuple-element.7857) | copy-start | bytes 12292
  818.2 1.4 copy-start.21
  818.6 98.3 %copy-start.3 = (f32[32,32]{1,0:T(8,128)S(1)}, f32[32,32]{1,0:T(8,128)}, u32[]{:S(2)}) copy-start(f32[32,32]{1,0:T(8,128)} %copy-done) | copy-start | bytes 12292
  819.6 184.9 %copy-start.20 = (f32[32,32]{0,1:T(8,128)S(1)}, f32[32,32]{0,1:T(8,128)}, u32[]{:S(2)}) copy-start(f32[32,32]{0,1:T(8,128)} %custom-call.8) | copy-start | bytes 12292
  906.2 143.3 %copy-start.4 = (f32[32,32]{1,0:T(8,128)S(1)}, f32[32,32]{1,0:T(8,128)}, u32[]{:S(2)}) copy-start(f32[32,32]{1,0:T(8,128)} %copy-done) | copy-start | bytes 12292
  1003.3 90.8 %copy-start.19 = (f32[32,32]{0,1:T(8,128)S(1)}, f32[32,32]{0,1:T(8,128)}, u32[]{:S(2)}) copy-start(f32[32,32]{0,1:T(8,128)} %custom-call.10) | copy-start | bytes 12292
  1003.7 135.5 %copy-start.5 = (f32[32,32]{1,0:T(8,128)S(1)}, f32[32,32]{1,0:T(8,128)}, u32[]{:S(2)}) copy-start(f32[32,32]{1,0:T(8,128)} %copy-done) | copy-start | bytes 12292
  1093.1 90.7 %copy-start.18 = (f32[32,32]{0,1:T(8,128)S(1)}, f32[32,32]{0,1:T(8,128)}, u32[]{:S(2)}) copy-start(f32[32,32]{0,1:T(8,128)} %custom-call.12) | copy-start | bytes 12292
  1093.4 135.4 %copy-start.6 = (f32[32,32]{1,0:T(8,128)S(1)}, f32[32,32]{1,0:T(8,128)}, u32[]{:S(2)}) copy-start(f32[32,32]{1,0:T(8,128)} %copy-done) | copy-start | bytes 12292
  1139.2 134.2 %copy-start.17 = (f32[32,32]{0,1:T(8,128)S(1)}, f32[32,32]{0,1:T(8,128)}, u32[]{:S(2)}) copy-start(f32[32,32]{0,1:T(8,128)} %custom-call.14) | copy-start | bytes 12292
  1183.0 143.6 %copy-start.7 = (f32[32,32]{1,0:T(8,128)S(1)}, f32[32,32]{1,0:T(8,128)}, u32[]{:S(2)}) copy-start(f32[32,32]{1,0:T(8,128)} %copy-done) | copy-start | bytes 12292
  1272.7 143.4 %copy-start.8 = (f32[32,32]{1,0:T(8,128)S(1)}, f32[32,32]{1,0:T(8,128)}, u32[]{:S(2)}) copy-start(f32[32,32]{1,0:T(8,128)} %copy-done) | copy-start | bytes 12292
  1322.9 182.6 %copy-start.9 = (f32[32,32]{1,0:T(8,128)S(1)}, f32[32,32]{1,0:T(8,128)}, u32[]{:S(2)}) copy-start(f32[32,32]{1,0:T(8,128)} %copy-done) | copy-start | bytes 12292
  1371.0 223.8 %copy-start.10 = (f32[32,32]{1,0:T(8,128)S(1)}, f32[32,32]{1,0:T(8,128)}, u32[]{:S(2)}) copy-start(f32[32,32]{1,0:T(8,128)} %copy-done) | copy-start | bytes 12292
  1505.5 186.3 %copy-start.11 = (f32[32,32]{1,0:T(8,128)S(1)}, f32[32,32]{1,0:T(8,128)}, u32[]{:S(2)}) copy-start(f32[32,32]{1,0:T(8,128)} %copy-done) | copy-start | bytes 12292
  1549.8 231.2 %copy-start.12 = (f32[32,32]{1,0:T(8,128)S(1)}, f32[32,32]{1,0:T(8,128)}, u32[]{:S(2)}) copy-start(f32[32,32]{1,0:T(8,128)} %copy-done) | copy-start | bytes 12292
  1638.7 231.5 %copy-start.13 = (f32[32,32]{1,0:T(8,128)S(1)}, f32[32,32]{1,0:T(8,128)}, u32[]{:S(2)}) copy-start(f32[32,32]{1,0:T(8,128)} %copy-done) | copy-start | bytes 12292
  1691.8 267.6 %copy-start.14 = (f32[32,32]{1,0:T(8,128)S(1)}, f32[32,32]{1,0:T(8,128)}, u32[]{:S(2)}) copy-start(f32[32,32]{1,0:T(8,128)} %copy-done) | copy-start | bytes 12292
  1913.8 102.7 %copy-start.23 = (f32[32,32]{0,1:T(8,128)S(1)}, f32[32,32]{0,1:T(8,128)}, u32[]{:S(2)}) copy-start(f32[32,32]{0,1:T(8,128)} %custom-call.30) | copy-start | bytes 12292
  1959.4 102.1 %copy-start.1 = (f32[32,32]{1,0:T(8,128)S(1)}, f32[32,32]{1,0:T(8,128)}, u32[]{:S(2)}) copy-start(f32[32,32]{1,0:T(8,128)} %copy-done) | copy-start | bytes 12292
  2133.2 0.7 copy-start.25
Sparse Core Ops, SparseCore 0:
  66.2 479.6 all-reduce.3
where the time goes:
time: 2160 us; the launch traced here: 2140 us
  local copies, waits for them, and re-layouts  667 us (31%)
  other arithmetic  500 us (23%)
  loops' own time  382 us (18%)
  waiting for transfers between devices  371 us (17%)
  blocking collectives  144 us (7%)
  matrix products  56.1 us (3%)
    another operation x16, loops' own time, small_factor(): lax.fori_loop(0, order, column_step, (matrix, jnp.zeros_like(matrix)))[1]  369 us
    psum x1, waiting for transfers between devices, shards(): gram_block, projected = lax.psum((gram_block, projected), ('rows', 'cols'))  368 us
    mul x1024, other arithmetic, row_step(): rest = rest - below[:, None] * value  363 us
    dynamic_slice x512, local copies, waits for them, and re-layouts, row_step(): pivot = lax.dynamic_slice_in_dim(column, index_row, 1, 0)[0]  322 us
    dynamic_slice x512, local copies, waits for them, and re-layouts, column_step(): pivot = jnp.sqrt(lax.dynamic_slice_in_dim(column, index_col, 1, 0)[0])  301 us
    psum x1, blocking collectives, shards(): gram_block, projected = lax.psum((gram_block, projected), ('rows', 'cols'))  110 us
    select_n x512, other arithmetic, column_step(): lower = jnp.where(positions[None, :] == index_col, column[:, None], lower)  80.9 us
    dot_general x123, matrix products, matmul(): jnp.dot(left, right, precision=lax.Precision.HIGHEST, preferred_element_t...  46.5 us

commit v1 on v0

--- a/solution.py
+++ b/solution.py
@@ -156,7 +156,7 @@
         leading, row_major, (((0,), (0,)), ((), ())), preferred_element_type=jnp.float32
     )
     projected = jnp.dot(grad_part, leading, preferred_element_type=jnp.float32)
-    gram_block, projected = lax.psum((gram_block, projected), ("rows", "cols"))
+    gram_block, projected = lax.psum(lax.psum((gram_block, projected), "cols"), "rows")
     gram_head = gram_block[:, :factored]
     gram_own = lax.dynamic_slice_in_dim(
         gram_block, lax.axis_index("cols") * cols_here, cols_here, 1

time: 2160 us -> 2040 us (0.944)
  waiting for transfers between devices: 371 us -> 228 us
    psum x1 -> x2, waiting for transfers between devices: 368 us -> 225 us  [the longest x1 142 us: shards(): lax.psum(lax.psum((gram_block, projected), 'cols'), 'rows')]
    psum x1 -> x2, blocking collectives: 110 us -> 131 us  [the longest x1 117 us: shards(): lax.psum(lax.psum((gram_block, projected), 'cols'), 'rows')]
where the time goes in v1:
time: 2040 us; the launch traced here: 2020 us
  local copies, waits for them, and re-layouts  667 us (33%)
  other arithmetic  500 us (25%)
  loops' own time  383 us (19%)
  waiting for transfers between devices  228 us (11%)
  blocking collectives  165 us (8%)
  matrix products  56.1 us (3%)
    another operation x16, loops' own time, small_factor(): lax.fori_loop(0, order, column_step, (matrix, jnp.zeros_like(matrix)))[1]  370 us
    mul x1024, other arithmetic, row_step(): rest = rest - below[:, None] * value  363 us
    dynamic_slice x512, local copies, waits for them, and re-layouts, row_step(): pivot = lax.dynamic_slice_in_dim(column, index_row, 1, 0)[0]  322 us
    dynamic_slice x512, local copies, waits for them, and re-layouts, column_step(): pivot = jnp.sqrt(lax.dynamic_slice_in_dim(column, index_col, 1, 0)[0])  302 us
    psum x1, waiting for transfers between devices, shards(): lax.psum(lax.psum((gram_block, projected), 'cols'), 'rows')  142 us
    psum x1, blocking collectives, shards(): lax.psum(lax.psum((gram_block, projected), 'cols'), 'rows')  117 us
    psum x1, waiting for transfers between devices, shards(): lax.psum((gram_block, projected), 'cols')  82.7 us
    select_n x512, other arithmetic, column_step(): lower = jnp.where(positions[None, :] == index_col, column[:, None], lower)  80.8 us

profile of v1, /device:TPU:1, one launch (start us, length us, event | category | flops | bytes accessed | tf_op | source)
XLA Modules:
  0.0 2020.3 jit_solution(425480406392088772)
XLA Ops:
  8.1 4.0 collective-permute-start
  13.5 2.9 collective-permute-done.1
  18.4 6.7 fusion.98
  25.0 2.9 copy.37
  27.9 34.2 %all_to_all.19 = bf16[8,1024,128]{1,2,0:T(8,128)(2,1)S(1)} all-to-all(bf16[8,1024,128]{1,2,0:T(8,128)(2,1)S(1)} %copy.37), channel_id=1, replica_groups=mesh['rows'=64,'cols'=8] {'cols'}, dimensions={0} | all-to-all | bytes 4194304 | tf_op jit(solution)/shard_map/all_to_all | solution.py:149
  63.4 2.6 fusion.161
  66.1 82.7 %all-reduce.5.cloned.1.call-done = f32[512,1024]{1,0:T(8,128)} async-done(((f32[512,1024]{1,0:T(8,128)}), f32[512,1024]{1,0:T(8,128)}) %all-reduce.5.cloned.1.call-update) | async-done | bytes 2097168 | tf_op jit(solution)/shard_map/psum | solution.py:159
  149.6 14.2 psum.30
  163.8 117.0 %psum.31 = f32[512]{0:T(512)S(1)} all-reduce(f32[512]{0:T(512)S(1)} %psum.30), channel_id=1, replica_groups=mesh['rows'=64,'cols'=8] {'rows'}, use_global_device_ids=true, to_apply=%region_67.68 | all-reduce | flops 512 | bytes 4096 | tf_op jit(solution)/shard_map/psum | solution.py:159
  280.8 142.4 %all-reduce.7.cloned.1.call-done = f32[512,1024]{1,0:T(8,128)} async-done(((f32[512,1024]{1,0:T(8,128)}), f32[512,1024]{1,0:T(8,128)}) %all-reduce.7.cloned.1.call-update) | async-done | bytes 2097168 | tf_op jit(solution)/shard_map/psum | solution.py:159
  423.9 47.9 %while.671 = (s32[]{:T(128)}, f32[32,32]{0,1:T(8,128)S(1)}, f32[32,32]{0,1:T(8,128)S(1)}, s32[]{:T(128)}, s32[]{:T(128)}, /*index=5*/s32[]{:T(128)}) while((s32[]{:T(128)}, f32[32,32]{0,1:T(8,128)S(1)}, f32[32,32]{0,1:T(8,128)S(1)}, s32[]{:T(128)}, s32[]{:T(128)}, /*index=5*/s32[]{:T(128)}) %tuple.1741), condition=%wide.region_3.4_spmd.clone.clone, body=%wide.region_2.3_spmd.clone.clone.sunk | while | flops 4292 | bytes 19003 | solution.py:60
  471.8 43.6 %while.672 = (s32[]{:T(128)}, f32[32,32]{1,0:T(8,128)S(1)}, f32[32,32]{1,0:T(8,128)S(1)}, f32[32,32]{0,1:T(8,128)S(1)}, s32[]{:T(128)}, /*index=5*/s32[]{:T(128)}, s32[]{:T(128)}) while((s32[]{:T(128)}, f32[32,32]{1,0:T(8,128)S(1)}, f32[32,32]{1,0:T(8,128)S(1)}, f32[32,32]{0,1:T(8,128)S(1)}, s32[]{:T(128)}, ...), condition=%wide.region_5.6_spmd.clone.clone, body=%wide.region_4.5_spmd.clone.clone.sunk | while | flops 4228 | bytes 18367 | solution.py:78
  516.8 2.3 convolution_subtract_fusion
  519.2 45.0 %while.673 = (s32[]{:T(128)}, f32[32,32]{0,1:T(8,128)S(1)}, f32[32,32]{0,1:T(8,128)S(1)}, s32[]{:T(128)}, s32[]{:T(128)}, /*index=5*/s32[]{:T(128)}) while((s32[]{:T(128)}, f32[32,32]{0,1:T(8,128)S(1)}, f32[32,32]{0,1:T(8,128)S(1)}, s32[]{:T(128)}, s32[]{:T(128)}, /*index=5*/s32[]{:T(128)}) %tuple.1747), condition=%wide.region_7.8_spmd.clone.clone, body=%wide.region_6.7_spmd.clone.clone.sunk | while | flops 4292 | bytes 19003 | solution.py:60
  564.2 43.6 %while.674 = (s32[]{:T(128)}, f32[32,32]{1,0:T(8,128)S(1)}, f32[32,32]{1,0:T(8,128)S(1)}, f32[32,32]{0,1:T(8,128)S(1)}, s32[]{:T(128)}, /*index=5*/s32[]{:T(128)}, s32[]{:T(128)}) while((s32[]{:T(128)}, f32[32,32]{1,0:T(8,128)S(1)}, f32[32,32]{1,0:T(8,128)S(1)}, f32[32,32]{0,1:T(8,128)S(1)}, s32[]{:T(128)}, ...), condition=%wide.region_9.10_spmd.clone.clone, body=%wide.region_8.9_spmd.clone.clone.sunk | while | flops 4228 | bytes 18367 | solution.py:78
  609.2 45.0 %while.675 = (s32[]{:T(128)}, f32[32,32]{0,1:T(8,128)S(1)}, f32[32,32]{0,1:T(8,128)S(1)}, s32[]{:T(128)}, s32[]{:T(128)}, /*index=5*/s32[]{:T(128)}) while((s32[]{:T(128)}, f32[32,32]{0,1:T(8,128)S(1)}, f32[32,32]{0,1:T(8,128)S(1)}, s32[]{:T(128)}, s32[]{:T(128)}, /*index=5*/s32[]{:T(128)}) %tuple.1753), condition=%wide.region_11.12_spmd.clone.clone, body=%wide.region_10.11_spmd.clone.clone.sunk | while | flops 4292 | bytes 19003 | solution.py:60
  654.2 43.6 %while.676 = (s32[]{:T(128)}, f32[32,32]{1,0:T(8,128)S(1)}, f32[32,32]{1,0:T(8,128)S(1)}, f32[32,32]{0,1:T(8,128)S(1)}, s32[]{:T(128)}, /*index=5*/s32[]{:T(128)}, s32[]{:T(128)}) while((s32[]{:T(128)}, f32[32,32]{1,0:T(8,128)S(1)}, f32[32,32]{1,0:T(8,128)S(1)}, f32[32,32]{0,1:T(8,128)S(1)}, s32[]{:T(128)}, ...), condition=%wide.region_13.14_spmd.clone.clone, body=%wide.region_12.13_spmd.clone.clone.sunk | while | flops 4228 | bytes 18367 | solution.py:78
  699.2 86.5 %while.677 = (s32[]{:T(128)}, f32[32,32]{0,1:T(8,128)S(1)}, f32[32,32]{0,1:T(8,128)}, s32[]{:T(128)}, s32[]{:T(128)}, /*index=5*/s32[]{:T(128)}) while((s32[]{:T(128)}, f32[32,32]{0,1:T(8,128)S(1)}, f32[32,32]{0,1:T(8,128)}, s32[]{:T(128)}, s32[]{:T(128)}, /*index=5*/s32[]{:T(128)}) %tuple.1759), condition=%wide.region_15.16_spmd.clone.clone, body=%wide.region_14.15_spmd.clone.clone.sunk | while | flops 4292 | bytes 19003 | solution.py:60
  785.9 1.4 scatter.101
  787.3 2.1 scatter.104
  790.8 2.1 scatter.106
  792.9 1.4 scatter.109
  794.3 2.1 scatter.110
  796.5 86.4 %while.678 = (s32[]{:T(128)}, f32[32,32]{1,0:T(8,128)S(1)}, f32[32,32]{1,0:T(8,128)S(1)}, f32[32,32]{0,1:T(8,128)}, s32[]{:T(128)}, /*index=5*/s32[]{:T(128)}, s32[]{:T(128)}) while((s32[]{:T(128)}, f32[32,32]{1,0:T(8,128)S(1)}, f32[32,32]{1,0:T(8,128)S(1)}, f32[32,32]{0,1:T(8,128)}, s32[]{:T(128)}, ...), condition=%wide.region_17.18_spmd.clone.clone, body=%wide.region_16.17_spmd.clone.clone.sunk | while | flops 4228 | bytes 18751 | solution.py:78
  884.0 45.0 %while.679 = (s32[]{:T(128)}, f32[32,32]{0,1:T(8,128)S(1)}, f32[32,32]{0,1:T(8,128)S(1)}, s32[]{:T(128)}, s32[]{:T(128)}, /*index=5*/s32[]{:T(128)}) while((s32[]{:T(128)}, f32[32,32]{0,1:T(8,128)S(1)}, f32[32,32]{0,1:T(8,128)S(1)}, s32[]{:T(128)}, s32[]{:T(128)}, /*index=5*/s32[]{:T(128)}) %tuple.1858), condition=%wide.region_19.20_spmd.clone.clone, body=%wide.region_18.19_spmd.clone.clone.sunk | while | flops 4292 | bytes 19003 | solution.py:60
  929.0 43.6 %while.680 = (s32[]{:T(128)}, f32[32,32]{1,0:T(8,128)S(1)}, f32[32,32]{1,0:T(8,128)S(1)}, f32[32,32]{0,1:T(8,128)S(1)}, s32[]{:T(128)}, /*index=5*/s32[]{:T(128)}, s32[]{:T(128)}) while((s32[]{:T(128)}, f32[32,32]{1,0:T(8,128)S(1)}, f32[32,32]{1,0:T(8,128)S(1)}, f32[32,32]{0,1:T(8,128)S(1)}, s32[]{:T(128)}, ...), condition=%wide.region_21.22_spmd.clone.clone, body=%wide.region_20.21_spmd.clone.clone.sunk | while | flops 4228 | bytes 18367 | solution.py:78
  973.7 45.0 %while.681 = (s32[]{:T(128)}, f32[32,32]{0,1:T(8,128)S(1)}, f32[32,32]{0,1:T(8,128)S(1)}, s32[]{:T(128)}, s32[]{:T(128)}, /*index=5*/s32[]{:T(128)}) while((s32[]{:T(128)}, f32[32,32]{0,1:T(8,128)S(1)}, f32[32,32]{0,1:T(8,128)S(1)}, s32[]{:T(128)}, s32[]{:T(128)}, /*index=5*/s32[]{:T(128)}) %tuple.1857), condition=%wide.region_23.24_spmd.clone.clone, body=%wide.region_22.23_spmd.clone.clone.sunk | while | flops 4292 | bytes 19003 | solution.py:60
  1018.7 43.6 %while.682 = (s32[]{:T(128)}, f32[32,32]{1,0:T(8,128)S(1)}, f32[32,32]{1,0:T(8,128)S(1)}, f32[32,32]{0,1:T(8,128)S(1)}, s32[]{:T(128)}, /*index=5*/s32[]{:T(128)}, s32[]{:T(128)}) while((s32[]{:T(128)}, f32[32,32]{1,0:T(8,128)S(1)}, f32[32,32]{1,0:T(8,128)S(1)}, f32[32,32]{0,1:T(8,128)S(1)}, s32[]{:T(128)}, ...), condition=%wide.region_25.26_spmd.clone.clone, body=%wide.region_24.25_spmd.clone.clone.sunk | while | flops 4228 | bytes 18367 | solution.py:78
  1063.3 45.0 %while.683 = (s32[]{:T(128)}, f32[32,32]{0,1:T(8,128)S(1)}, f32[32,32]{0,1:T(8,128)S(1)}, s32[]{:T(128)}, s32[]{:T(128)}, /*index=5*/s32[]{:T(128)}) while((s32[]{:T(128)}, f32[32,32]{0,1:T(8,128)S(1)}, f32[32,32]{0,1:T(8,128)S(1)}, s32[]{:T(128)}, s32[]{:T(128)}, /*index=5*/s32[]{:T(128)}) %tuple.1856), condition=%wide.region_27.28_spmd.clone.clone, body=%wide.region_26.27_spmd.clone.clone.sunk | while | flops 4292 | bytes 19003 | solution.py:60
  1108.3 43.6 %while.684 = (s32[]{:T(128)}, f32[32,32]{1,0:T(8,128)S(1)}, f32[32,32]{1,0:T(8,128)S(1)}, f32[32,32]{0,1:T(8,128)S(1)}, s32[]{:T(128)}, /*index=5*/s32[]{:T(128)}, s32[]{:T(128)}) while((s32[]{:T(128)}, f32[32,32]{1,0:T(8,128)S(1)}, f32[32,32]{1,0:T(8,128)S(1)}, f32[32,32]{0,1:T(8,128)S(1)}, s32[]{:T(128)}, ...), condition=%wide.region_29.30_spmd.clone.clone, body=%wide.region_28.29_spmd.clone.clone.sunk | while | flops 4228 | bytes 18367 | solution.py:78
  1152.9 45.0 %while.685 = (s32[]{:T(128)}, f32[32,32]{0,1:T(8,128)S(1)}, f32[32,32]{0,1:T(8,128)S(1)}, s32[]{:T(128)}, s32[]{:T(128)}, /*index=5*/s32[]{:T(128)}) while((s32[]{:T(128)}, f32[32,32]{0,1:T(8,128)S(1)}, f32[32,32]{0,1:T(8,128)S(1)}, s32[]{:T(128)}, s32[]{:T(128)}, /*index=5*/s32[]{:T(128)}) %tuple.1855), condition=%wide.region_31.32_spmd.clone.clone, body=%wide.region_30.31_spmd.clone.clone.sunk | while | flops 4292 | bytes 19003 | solution.py:60
  1206.1 43.6 %while.686 = (s32[]{:T(128)}, f32[32,32]{1,0:T(8,128)S(1)}, f32[32,32]{1,0:T(8,128)S(1)}, f32[32,32]{0,1:T(8,128)S(1)}, s32[]{:T(128)}, /*index=5*/s32[]{:T(128)}, s32[]{:T(128)}) while((s32[]{:T(128)}, f32[32,32]{1,0:T(8,128)S(1)}, f32[32,32]{1,0:T(8,128)S(1)}, f32[32,32]{0,1:T(8,128)S(1)}, s32[]{:T(128)}, ...), condition=%wide.region_33.34_spmd.clone.clone, body=%wide.region_32.33_spmd.clone.clone.sunk | while | flops 4228 | bytes 18367 | solution.py:78
  1250.5 45.0 %while.687 = (s32[]{:T(128)}, f32[32,32]{0,1:T(8,128)S(1)}, f32[32,32]{0,1:T(8,128)S(1)}, s32[]{:T(128)}, s32[]{:T(128)}, /*index=5*/s32[]{:T(128)}) while((s32[]{:T(128)}, f32[32,32]{0,1:T(8,128)S(1)}, f32[32,32]{0,1:T(8,128)S(1)}, s32[]{:T(128)}, s32[]{:T(128)}, /*index=5*/s32[]{:T(128)}) %tuple.1789), condition=%wide.region_35.36_spmd.clone.clone, body=%wide.region_34.35_spmd.clone.clone.sunk | while | flops 4292 | bytes 19003 | solution.py:60
  1295.6 43.6 %while.688 = (s32[]{:T(128)}, f32[32,32]{1,0:T(8,128)S(1)}, f32[32,32]{1,0:T(8,128)S(1)}, f32[32,32]{0,1:T(8,128)S(1)}, s32[]{:T(128)}, /*index=5*/s32[]{:T(128)}, s32[]{:T(128)}) while((s32[]{:T(128)}, f32[32,32]{1,0:T(8,128)S(1)}, f32[32,32]{1,0:T(8,128)S(1)}, f32[32,32]{0,1:T(8,128)S(1)}, s32[]{:T(128)}, ...), condition=%wide.region_37.38_spmd.clone.clone, body=%wide.region_36.37_spmd.clone.clone.sunk | while | flops 4228 | bytes 18367 | solution.py:78
  1340.0 45.0 %while.689 = (s32[]{:T(128)}, f32[32,32]{0,1:T(8,128)S(1)}, f32[32,32]{0,1:T(8,128)S(1)}, s32[]{:T(128)}, s32[]{:T(128)}, /*index=5*/s32[]{:T(128)}) while((s32[]{:T(128)}, f32[32,32]{0,1:T(8,128)S(1)}, f32[32,32]{0,1:T(8,128)S(1)}, s32[]{:T(128)}, s32[]{:T(128)}, /*index=5*/s32[]{:T(128)}) %tuple.1795), condition=%wide.region_39.40_spmd.clone.clone, body=%wide.region_38.39_spmd.clone.clone.sunk | while | flops 4292 | bytes 19003 | solution.py:60
  1385.0 43.6 %while.690 = (s32[]{:T(128)}, f32[32,32]{1,0:T(8,128)S(1)}, f32[32,32]{1,0:T(8,128)S(1)}, f32[32,32]{0,1:T(8,128)S(1)}, s32[]{:T(128)}, /*index=5*/s32[]{:T(128)}, s32[]{:T(128)}) while((s32[]{:T(128)}, f32[32,32]{1,0:T(8,128)S(1)}, f32[32,32]{1,0:T(8,128)S(1)}, f32[32,32]{0,1:T(8,128)S(1)}, s32[]{:T(128)}, ...), condition=%wide.region_41.42_spmd.clone.clone, body=%wide.region_40.41_spmd.clone.clone.sunk | while | flops 4228 | bytes 18367 | solution.py:78
  1429.3 45.0 %while.691 = (s32[]{:T(128)}, f32[32,32]{0,1:T(8,128)S(1)}, f32[32,32]{0,1:T(8,128)S(1)}, s32[]{:T(128)}, s32[]{:T(128)}, /*index=5*/s32[]{:T(128)}) while((s32[]{:T(128)}, f32[32,32]{0,1:T(8,128)S(1)}, f32[32,32]{0,1:T(8,128)S(1)}, s32[]{:T(128)}, s32[]{:T(128)}, /*index=5*/s32[]{:T(128)}) %tuple.1801), condition=%wide.region_43.44_spmd.clone.clone, body=%wide.region_42.43_spmd.clone.clone.sunk | while | flops 4292 | bytes 19003 | solution.py:60
  1474.4 43.6 %while.692 = (s32[]{:T(128)}, f32[32,32]{1,0:T(8,128)S(1)}, f32[32,32]{1,0:T(8,128)S(1)}, f32[32,32]{0,1:T(8,128)S(1)}, s32[]{:T(128)}, /*index=5*/s32[]{:T(128)}, s32[]{:T(128)}) while((s32[]{:T(128)}, f32[32,32]{1,0:T(8,128)S(1)}, f32[32,32]{1,0:T(8,128)S(1)}, f32[32,32]{0,1:T(8,128)S(1)}, s32[]{:T(128)}, ...), condition=%wide.region_45.46_spmd.clone.clone, body=%wide.region_44.45_spmd.clone.clone.sunk | while | flops 4228 | bytes 18367 | solution.py:78
  1518.7 45.0 %while.693 = (s32[]{:T(128)}, f32[32,32]{0,1:T(8,128)S(1)}, f32[32,32]{0,1:T(8,128)S(1)}, s32[]{:T(128)}, s32[]{:T(128)}, /*index=5*/s32[]{:T(128)}) while((s32[]{:T(128)}, f32[32,32]{0,1:T(8,128)S(1)}, f32[32,32]{0,1:T(8,128)S(1)}, s32[]{:T(128)}, s32[]{:T(128)}, /*index=5*/s32[]{:T(128)}) %tuple.1807), condition=%wide.region_47.48_spmd.clone.clone, body=%wide.region_46.47_spmd.clone.clone.sunk | while | flops 4292 | bytes 19003 | solution.py:60
  1571.3 43.6 %while.694 = (s32[]{:T(128)}, f32[32,32]{1,0:T(8,128)S(1)}, f32[32,32]{1,0:T(8,128)S(1)}, f32[32,32]{0,1:T(8,128)S(1)}, s32[]{:T(128)}, /*index=5*/s32[]{:T(128)}, s32[]{:T(128)}) while((s32[]{:T(128)}, f32[32,32]{1,0:T(8,128)S(1)}, f32[32,32]{1,0:T(8,128)S(1)}, f32[32,32]{0,1:T(8,128)S(1)}, s32[]{:T(128)}, ...), condition=%wide.region_49.50_spmd.clone.clone, body=%wide.region_48.49_spmd.clone.clone.sunk | while | flops 4228 | bytes 18367 | solution.py:78
  1615.5 45.0 %while.695 = (s32[]{:T(128)}, f32[32,32]{0,1:T(8,128)S(1)}, f32[32,32]{0,1:T(8,128)S(1)}, s32[]{:T(128)}, s32[]{:T(128)}, /*index=5*/s32[]{:T(128)}) while((s32[]{:T(128)}, f32[32,32]{0,1:T(8,128)S(1)}, f32[32,32]{0,1:T(8,128)S(1)}, s32[]{:T(128)}, s32[]{:T(128)}, /*index=5*/s32[]{:T(128)}) %tuple.1813), condition=%wide.region_51.52_spmd.clone.clone, body=%wide.region_50.51_spmd.clone.clone.sunk | while | flops 4292 | bytes 19003 | solution.py:60
  1660.5 43.6 %while.696 = (s32[]{:T(128)}, f32[32,32]{1,0:T(8,128)S(1)}, f32[32,32]{1,0:T(8,128)S(1)}, f32[32,32]{0,1:T(8,128)S(1)}, s32[]{:T(128)}, /*index=5*/s32[]{:T(128)}, s32[]{:T(128)}) while((s32[]{:T(128)}, f32[32,32]{1,0:T(8,128)S(1)}, f32[32,32]{1,0:T(8,128)S(1)}, f32[32,32]{0,1:T(8,128)S(1)}, s32[]{:T(128)}, ...), condition=%wide.region_53.54_spmd.clone.clone, body=%wide.region_52.53_spmd.clone.clone.sunk | while | flops 4228 | bytes 18367 | solution.py:78
  1704.7 45.0 %while.697 = (s32[]{:T(128)}, f32[32,32]{0,1:T(8,128)S(1)}, f32[32,32]{0,1:T(8,128)S(1)}, s32[]{:T(128)}, s32[]{:T(128)}, /*index=5*/s32[]{:T(128)}) while((s32[]{:T(128)}, f32[32,32]{0,1:T(8,128)S(1)}, f32[32,32]{0,1:T(8,128)S(1)}, s32[]{:T(128)}, s32[]{:T(128)}, /*index=5*/s32[]{:T(128)}) %tuple.1819), condition=%wide.region_55.56_spmd.clone.clone, body=%wide.region_54.55_spmd.clone.clone.sunk | while | flops 4292 | bytes 19003 | solution.py:60
  1749.7 43.6 %while.698 = (s32[]{:T(128)}, f32[32,32]{1,0:T(8,128)S(1)}, f32[32,32]{1,0:T(8,128)S(1)}, f32[32,32]{0,1:T(8,128)S(1)}, s32[]{:T(128)}, /*index=5*/s32[]{:T(128)}, s32[]{:T(128)}) while((s32[]{:T(128)}, f32[32,32]{1,0:T(8,128)S(1)}, f32[32,32]{1,0:T(8,128)S(1)}, f32[32,32]{0,1:T(8,128)S(1)}, s32[]{:T(128)}, ...), condition=%wide.region_57.58_spmd.clone.clone, body=%wide.region_56.57_spmd.clone.clone.sunk | while | flops 4228 | bytes 18367 | solution.py:78
  1793.8 45.0 %while.699 = (s32[]{:T(128)}, f32[32,32]{0,1:T(8,128)S(1)}, f32[32,32]{0,1:T(8,128)S(1)}, s32[]{:T(128)}, s32[]{:T(128)}, /*index=5*/s32[]{:T(128)}) while((s32[]{:T(128)}, f32[32,32]{0,1:T(8,128)S(1)}, f32[32,32]{0,1:T(8,128)S(1)}, s32[]{:T(128)}, s32[]{:T(128)}, /*index=5*/s32[]{:T(128)}) %tuple.1825), condition=%wide.region_59.60_spmd.clone.clone, body=%wide.region_58.59_spmd.clone.clone.sunk | while | flops 4292 | bytes 19003 | solution.py:60
  1838.9 43.6 %while.700 = (s32[]{:T(128)}, f32[32,32]{1,0:T(8,128)S(1)}, f32[32,32]{1,0:T(8,128)S(1)}, f32[32,32]{0,1:T(8,128)S(1)}, s32[]{:T(128)}, /*index=5*/s32[]{:T(128)}, s32[]{:T(128)}) while((s32[]{:T(128)}, f32[32,32]{1,0:T(8,128)S(1)}, f32[32,32]{1,0:T(8,128)S(1)}, f32[32,32]{0,1:T(8,128)S(1)}, s32[]{:T(128)}, ...), condition=%wide.region_61.62_spmd.clone.clone, body=%wide.region_60.61_spmd.clone.clone.sunk | while | flops 4228 | bytes 18367 | solution.py:78
  1896.0 45.0 %while.701 = (s32[]{:T(128)}, f32[32,32]{0,1:T(8,128)S(1)}, f32[32,32]{0,1:T(8,128)S(1)}, s32[]{:T(128)}, s32[]{:T(128)}, /*index=5*/s32[]{:T(128)}) while((s32[]{:T(128)}, f32[32,32]{0,1:T(8,128)S(1)}, f32[32,32]{0,1:T(8,128)S(1)}, s32[]{:T(128)}, s32[]{:T(128)}, /*index=5*/s32[]{:T(128)}) %tuple.1859), condition=%wide.region_63.64_spmd.clone.clone, body=%wide.region_62.63_spmd.clone.clone.sunk | while | flops 4292 | bytes 19003 | solution.py:60
  1941.0 43.6 %while.702 = (s32[]{:T(128)}, f32[32,32]{1,0:T(8,128)S(1)}, f32[32,32]{1,0:T(8,128)S(1)}, f32[32,32]{0,1:T(8,128)S(1)}, s32[]{:T(128)}, /*index=5*/s32[]{:T(128)}, s32[]{:T(128)}) while((s32[]{:T(128)}, f32[32,32]{1,0:T(8,128)S(1)}, f32[32,32]{1,0:T(8,128)S(1)}, f32[32,32]{0,1:T(8,128)S(1)}, s32[]{:T(128)}, ...), condition=%wide.region_65.66_spmd.clone.clone, body=%wide.region_64.65_spmd.clone.clone.sunk | while | flops 4228 | bytes 18367 | solution.py:78
  (5426 shorter events, 1200.5 us)
Async XLA Ops:
  7.2 141.7 %all-reduce.5.cloned.1.call-start = ((), (), s32[]{:S(2)}) async-start(), calls=%async_computation.1 | async-start | bytes 4194304 | tf_op jit(solution)/shard_map/psum | solution.py:159
  8.1 5.4 collective-permute-start
  12.1 4.4 collective-permute-start.1
  62.1 1.3 copy-start.15
  66.0 83.2 %copy-start.24 = (bf16[8,1024]{1,0:T(8,128)(2,1)S(1)}, bf16[8,1024]{1,0:T(8,128)(2,1)}, u32[]{:S(2)}) copy-start(bf16[8,1024]{1,0:T(8,128)(2,1)} %param.133) | copy-start | bytes 49156
  66.0 83.2 %copy-start.16 = (bf16[8,1024,128]{1,2,0:T(8,128)(2,1)S(1)}, bf16[8,1024,128]{1,2,0:T(8,128)(2,1)}, u32[]{:S(2)}) copy-start(bf16[8,1024,128]{1,2,0:T(8,128)(2,1)} %copy-done.15) | copy-start | bytes 6291460
  66.1 357.1 %all-reduce.7.cloned.1.call-start = ((), (), s32[]{:S(2)}) async-start(), calls=%async_computation.2 | async-start | bytes 4194304 | tf_op jit(solution)/shard_map/psum | solution.py:159
  148.9 370.2 %copy-start = (f32[32,32]{1,0:T(8,128)}, f32[32,32]{1,0:T(8,128)S(1)}, u32[]{:S(2)}) copy-start(f32[32,32]{1,0:T(8,128)S(1)} %fusion.258) | copy-start | bytes 12292
  519.1 135.1 %copy-start.2 = (f32[32,32]{1,0:T(8,128)S(1)}, f32[32,32]{1,0:T(8,128)}, u32[]{:S(2)}) copy-start(f32[32,32]{1,0:T(8,128)} %copy-done) | copy-start | bytes 12292
  607.8 91.3 %copy-start.22 = (f32[32,32]{0,1:T(8,128)}, f32[32,32]{0,1:T(8,128)S(1)}, u32[]{:S(2)}) copy-start(f32[32,32]{0,1:T(8,128)S(1)} %get-tuple-element.7861) | copy-start | bytes 12292
  697.8 1.4 copy-start.21
  698.2 98.2 %copy-start.3 = (f32[32,32]{1,0:T(8,128)S(1)}, f32[32,32]{1,0:T(8,128)}, u32[]{:S(2)}) copy-start(f32[32,32]{1,0:T(8,128)} %copy-done) | copy-start | bytes 12292
  699.2 184.8 %copy-start.20 = (f32[32,32]{0,1:T(8,128)S(1)}, f32[32,32]{0,1:T(8,128)}, u32[]{:S(2)}) copy-start(f32[32,32]{0,1:T(8,128)} %custom-call.8) | copy-start | bytes 12292
  785.7 143.2 %copy-start.4 = (f32[32,32]{1,0:T(8,128)S(1)}, f32[32,32]{1,0:T(8,128)}, u32[]{:S(2)}) copy-start(f32[32,32]{1,0:T(8,128)} %copy-done) | copy-start | bytes 12292
  882.9 90.8 %copy-start.19 = (f32[32,32]{0,1:T(8,128)S(1)}, f32[32,32]{0,1:T(8,128)}, u32[]{:S(2)}) copy-start(f32[32,32]{0,1:T(8,128)} %custom-call.10) | copy-start | bytes 12292
  883.2 135.5 %copy-start.5 = (f32[32,32]{1,0:T(8,128)S(1)}, f32[32,32]{1,0:T(8,128)}, u32[]{:S(2)}) copy-start(f32[32,32]{1,0:T(8,128)} %copy-done) | copy-start | bytes 12292
  972.6 90.7 %copy-start.18 = (f32[32,32]{0,1:T(8,128)S(1)}, f32[32,32]{0,1:T(8,128)}, u32[]{:S(2)}) copy-start(f32[32,32]{0,1:T(8,128)} %custom-call.12) | copy-start | bytes 12292
  972.9 135.4 %copy-start.6 = (f32[32,32]{1,0:T(8,128)S(1)}, f32[32,32]{1,0:T(8,128)}, u32[]{:S(2)}) copy-start(f32[32,32]{1,0:T(8,128)} %copy-done) | copy-start | bytes 12292
  1018.7 134.2 %copy-start.17 = (f32[32,32]{0,1:T(8,128)S(1)}, f32[32,32]{0,1:T(8,128)}, u32[]{:S(2)}) copy-start(f32[32,32]{0,1:T(8,128)} %custom-call.14) | copy-start | bytes 12292
  1062.6 143.6 %copy-start.7 = (f32[32,32]{1,0:T(8,128)S(1)}, f32[32,32]{1,0:T(8,128)}, u32[]{:S(2)}) copy-start(f32[32,32]{1,0:T(8,128)} %copy-done) | copy-start | bytes 12292
  1152.2 143.4 %copy-start.8 = (f32[32,32]{1,0:T(8,128)S(1)}, f32[32,32]{1,0:T(8,128)}, u32[]{:S(2)}) copy-start(f32[32,32]{1,0:T(8,128)} %copy-done) | copy-start | bytes 12292
  1202.4 182.6 %copy-start.9 = (f32[32,32]{1,0:T(8,128)S(1)}, f32[32,32]{1,0:T(8,128)}, u32[]{:S(2)}) copy-start(f32[32,32]{1,0:T(8,128)} %copy-done) | copy-start | bytes 12292
  1250.5 223.8 %copy-start.10 = (f32[32,32]{1,0:T(8,128)S(1)}, f32[32,32]{1,0:T(8,128)}, u32[]{:S(2)}) copy-start(f32[32,32]{1,0:T(8,128)} %copy-done) | copy-start | bytes 12292
  1385.0 186.3 %copy-start.11 = (f32[32,32]{1,0:T(8,128)S(1)}, f32[32,32]{1,0:T(8,128)}, u32[]{:S(2)}) copy-start(f32[32,32]{1,0:T(8,128)} %copy-done) | copy-start | bytes 12292
  1429.3 231.2 %copy-start.12 = (f32[32,32]{1,0:T(8,128)S(1)}, f32[32,32]{1,0:T(8,128)}, u32[]{:S(2)}) copy-start(f32[32,32]{1,0:T(8,128)} %copy-done) | copy-start | bytes 12292
  1518.2 231.5 %copy-start.13 = (f32[32,32]{1,0:T(8,128)S(1)}, f32[32,32]{1,0:T(8,128)}, u32[]{:S(2)}) copy-start(f32[32,32]{1,0:T(8,128)} %copy-done) | copy-start | bytes 12292
  1571.3 267.6 %copy-start.14 = (f32[32,32]{1,0:T(8,128)S(1)}, f32[32,32]{1,0:T(8,128)}, u32[]{:S(2)}) copy-start(f32[32,32]{1,0:T(8,128)} %copy-done) | copy-start | bytes 12292
  1793.3 102.7 %copy-start.23 = (f32[32,32]{0,1:T(8,128)S(1)}, f32[32,32]{0,1:T(8,128)}, u32[]{:S(2)}) copy-start(f32[32,32]{0,1:T(8,128)} %custom-call.30) | copy-start | bytes 12292
  1838.9 102.1 %copy-start.1 = (f32[32,32]{1,0:T(8,128)S(1)}, f32[32,32]{1,0:T(8,128)}, u32[]{:S(2)}) copy-start(f32[32,32]{1,0:T(8,128)} %copy-done) | copy-start | bytes 12292
  2012.7 0.7 copy-start.25
Sparse Core Ops, SparseCore 0:
  66.2 82.5 all-reduce.4
  152.2 270.8 all-reduce.6
